TPU v7x, 32 devices: a whole 2x2x4 slice. The times are simulated.
32 devices in a mesh: dp: 8 (over z, y), phase: 2 (over core), mp: 2 (over x).
Axes of the slice: x: 2, y: 2, z: 4, core: 2. Of those that a mesh axis runs over, the one named last changes fastest.
Arguments:
- sec_acts: bfloat16 [2, 8, 512, 4096], P('phase', 'dp', None, 'mp'), may hold values from -40 to 40
- gain: bfloat16 [4096], P('mp'), may hold values from 0.5 to 1.5
- w_kv: bfloat16 [4096, 4096], P(('dp', 'phase'), 'mp'), may hold values from -0.09375 to 0.09375
- src_len: int32 [8], P('dp'), may hold values from 1 to 512, 2560 in all
- tgt_len: int32 [8], P('dp'), may hold values from 1 to 512, 3072 in all
Outputs:
- sec_grads: bfloat16 [2, 8, 512, 4096], P('phase', 'dp', None, 'mp')
- d_wkv: float32 [4096, 4096], P(('dp', 'phase'), 'mp')
- d_gain: float32 [4096], P('mp')
Inputs may be any that keep to these rules, and one draw needn't show every extreme that they name: Source positions 0 to src_len - 1 of a pair are real, the rest padding; some pair has exactly 512. Target positions 0 to tgt_len - 1 of a pair carry loss, the rest padding; some pair has exactly 512.
All inputs are finite; a program needn't handle non-finite values. No bound on the sum of `src_len` or of `tgt_len` on one device may be relied on, other than what follows from the above.
Results may differ from a plain program's by a relative error of at most 0.022.
Values may be sent and summed in bfloat16 or wider, within the bound.
No kernel may reach another device: no remote copies, remote signals or barrier semaphores. Data moves between devices by JAX's collectives and lax.ppermute only.
A program may use at most 128 MiB of HBM per device.

v0:
```python
import jax
import jax.numpy as jnp
from jax import lax
from jax.sharding import PartitionSpec as P

D = 4096
HEAD = 64
norm_epsilon = 1e-06


def shifted(value, axis, steps):
    count = lax.axis_size(axis)
    initial, last = (max(0, -steps), min(count, count - steps))
    return lax.ppermute(value, axis, [(source, source + steps) for source in range(initial, last)])


def attend_back(queries, grad_out, key_heads, values, key_mask):
    f32 = jnp.float32
    bf16 = jnp.bfloat16
    factor = 1.0 / HEAD**0.5
    scores = factor * jnp.einsum("pihd,pjhd->phij", queries, key_heads, preferred_element_type=f32)
    scores = jnp.where(key_mask[:, None, None, :], scores, -1e30)
    row_top = jnp.max(scores, axis=-1, keepdims=True)
    weights = jnp.exp(scores - row_top)
    probability = weights / jnp.sum(weights, axis=-1, keepdims=True)
    prob_low = probability.astype(bf16)
    attended = jnp.einsum("phij,pjhd->pihd", prob_low, values, preferred_element_type=f32)
    grad_prob = jnp.einsum("pihd,pjhd->phij", grad_out, values, preferred_element_type=f32)
    row_delta = jnp.einsum("pihd,pihd->phi", grad_out.astype(f32), attended)
    grad_score = (factor * probability * (grad_prob - row_delta[..., None])).astype(bf16)
    grad_query = jnp.einsum(
        "phij,pjhd->pihd", grad_score, key_heads, preferred_element_type=f32
    ).astype(bf16)
    grad_key = jnp.einsum(
        "phij,pihd->pjhd", grad_score, queries, preferred_element_type=f32
    ).astype(bf16)
    grad_value = jnp.einsum(
        "phij,pihd->pjhd", prob_low, grad_out, preferred_element_type=f32
    ).astype(bf16)
    return (grad_query, grad_key, grad_value)


def on_device(sec_acts, gain, w_kv, src_len, tgt_len):
    f32 = jnp.float32
    bf16 = jnp.bfloat16
    section = lax.axis_index("phase")
    packed = sec_acts[0]
    pair_dev, length, shard_width = packed.shape
    row_count = pair_dev * length
    pair_total = pair_dev * lax.axis_size("dp")
    pair_scale = 1.0 / pair_total
    hidden = packed.astype(f32)
    squares = lax.psum(jnp.sum(hidden * hidden, axis=-1), "mp")
    inv_rms = lax.rsqrt(squares / D + norm_epsilon)[..., None]
    normed = hidden * inv_rms
    gain_wide = gain.astype(f32)
    enc_shard = (normed * gain_wide).astype(bf16)
    enc_moved = shifted(enc_shard, "phase", 1)
    enc_full = lax.all_gather(enc_moved, "mp", axis=2, tiled=True)
    enc_rows = enc_full.reshape(row_count, D)
    whole_weight = lax.all_gather(w_kv, ("dp", "phase"), axis=0, tiled=True)
    key_value = jnp.dot(enc_rows, whole_weight, preferred_element_type=f32)
    heads_dev = shard_width // (2 * HEAD)
    kv_split = key_value.astype(bf16).reshape(pair_dev, length, heads_dev, 2, HEAD)
    dec_split = packed.reshape(pair_dev, length, heads_dev, 2, HEAD)
    positions = jnp.arange(length, dtype=jnp.int32)
    query_mask = positions[None, :] < tgt_len[:, None]
    key_mask = positions[None, :] < src_len[:, None]
    grad_out = jnp.where(query_mask[:, :, None, None], dec_split[:, :, :, 1], jnp.zeros((), bf16))
    grad_query, grad_key, grad_value = attend_back(
        dec_split[:, :, :, 0], grad_out, kv_split[:, :, :, 0], kv_split[:, :, :, 1], key_mask
    )
    dec_grads = jnp.stack([grad_query, grad_key], axis=3).reshape(pair_dev, length, shard_width)
    grad_kv = jnp.stack([grad_key, grad_value], axis=3).reshape(row_count, shard_width)
    reduced = lax.psum_scatter(
        (
            pair_scale
            * lax.dot_general(
                enc_rows, grad_kv, (((0,), (0,)), ((), ())), preferred_element_type=f32
            )
        ).astype(jnp.bfloat16),
        "dp",
        scatter_dimension=0,
        tiled=True,
    ).astype(jnp.float32)
    half_rows = reduced.shape[0] // 2
    lower_rows = shifted(reduced[:half_rows], "phase", -1)
    d_wkv = jnp.where(section == 0, lower_rows, reduced[half_rows:])
    partial_enc = lax.dot_general(
        grad_kv, whole_weight, (((1,), (1,)), ((), ())), preferred_element_type=f32
    ).astype(bf16)
    partial_enc = partial_enc.reshape(1, pair_dev, length, D)
    pieces = lax.all_to_all(partial_enc, "mp", split_axis=3, concat_axis=0, tiled=True)
    summed = jnp.sum(pieces.astype(f32), axis=0)
    grad_enc = shifted(summed, "phase", -1)
    grad_normed = grad_enc * gain_wide
    gain_term = pair_scale * jnp.sum(grad_enc * normed, axis=(0, 1))
    d_gain = lax.psum(gain_term, ("dp", "phase"))
    sec_grads = jnp.where(section == 0, grad_normed.astype(bf16), dec_grads)[None]
    return (sec_grads, d_wkv, d_gain)


def solution(mesh):
    placed = (P("phase", "dp", None, "mp"), P("mp"), P(("dp", "phase"), "mp"), P("dp"), P("dp"))
    return jax.shard_map(
        on_device,
        mesh=mesh,
        in_specs=placed,
        out_specs=(P("phase", "dp", None, "mp"), P(("dp", "phase"), "mp"), P("mp")),
        check_vma=False,
    )
```

profile of v0, /device:TPU:0, one launch (start us, length us, event | category | flops | bytes accessed | tf_op | source)
XLA Modules:
  0.0 626.1 jit_solution(5916800260280279327)
XLA Ops:
  7.2 0.0 all-gather.3.cloned.1.call-start
  7.2 0.7 convert_element_type.108
  7.9 2.1 fusion.14
  10.0 0.0 copy-start
  10.0 6.0 psum.14
  16.0 2.1 fusion.12
  18.1 2.7 collective-permute-start
  20.8 2.5 collective-permute-done
  23.3 0.0 all-gather.3.cloned.1.call-update
  23.3 0.0 all-gather.5.cloned.1.call-start
  23.4 0.7 all-gather.5.cloned.1.call-update
  24.1 0.0 reduce-scatter.2.cloned.1.call-start
  24.1 0.0 copy-done
  24.1 2.5 copy.33
  28.0 54.1 %all-gather.3.cloned.1.call-done = bf16[1,512,4096]{2,1,0:T(8,128)(2,1)} async-done(((bf16[1,512,2048]{2,1,0:T(8,128)(2,1)}), bf16[1,512,4096]{2,1,0:T(8,128)(2,1)}) %all-gather.3.cloned.1.call-update) | async-done | bytes 4194320 | tf_op jit(solution)/shard_map/all_gather | solution.py:59
  82.1 129.1 %all-gather.5.cloned.1.call-done = bf16[4096,2048]{1,0:T(8,128)(2,1)} async-done(((bf16[256,2048]{1,0:T(8,128)(2,1)}), bf16[4096,2048]{1,0:T(8,128)(2,1)}) %all-gather.5.cloned.1.call-update) | async-done | bytes 16777232 | tf_op jit(solution)/shard_map/all_gather | solution.py:61
  211.2 14.5 %fusion.18 = bf16[512,2048]{1,0:T(8,128)(2,1)} fusion(bf16[4096,2048]{1,0:T(8,128)(2,1)} %all-gather.5.cloned.1.call-done, bf16[1,512,4096]{2,1,0:T(8,128)(2,1)} %all-gather.3.cloned.1.call-done), kind=kOutput, calls=%fused_computation.26 | convolution fusion | flops 8590983168 | bytes 23068672 | tf_op jit(solution)/shard_map/dot_general | solution.py:62
  225.7 3.9 copy.31
  229.6 11.0 %fusion.39 = (f32[16,512]{1,0:T(8,128)S(1)}, f32[16,512,512]{1,2,0:T(8,128)}) fusion(pred[512]{0:T(512)(128)(4,1)S(1)} %iota_compare_fusion.1, bf16[1,512,16,2,64]{1,4,3,2,0:T(8,128)(2,1)} %bitcast.131, bf16[1,512,16,2,64]{1,4,3,2,0:T(8,128)(2,1)} %bitcast.126), kind=kOutput, calls=%fused_computation.57 | convolution fusion | flops 553648640 | bytes 18907648 | tf_op jit(solution)/shard_map/sub | solution.py:24
  240.7 0.0 copy-start.1
  240.7 6.8 %fusion.8 = bf16[16,512,512]{1,2,0:T(8,128)(2,1)S(1)} fusion(f32[16,512,512]{1,2,0:T(8,128)} %get-tuple-element.9, f32[16,512]{1,0:T(8,128)S(1)} %get-tuple-element.8), kind=kLoop, calls=%fused_computation.12 | loop fusion | flops 8388608 | bytes 25198592 | tf_op jit(solution)/shard_map/convert_element_type | solution.py:26
  247.5 0.0 copy-done.1
  247.5 0.0 copy-start.2
  247.5 3.6 fusion.27
  251.2 0.0 copy-done.2
  251.2 1.5 fusion.23
  252.7 7.8 %multiply_convert_fusion.1 = bf16[16,512,512]{1,2,0:T(8,128)(2,1)S(1)} fusion(f32[16,512]{1,0:T(8,128)S(1)} %fusion.23, f32[16,512,512]{1,2,0:T(8,128)} %get-tuple-element.9, f32[16,512]{1,0:T(8,128)S(1)} %get-tuple-element.8, bf16[1,512,16,2,64]{1,4,3,2,0:T(8,128)(2,1)S(1)} %bitcast.133, bf16[1,512,16,2,64]{1,4,3,2,0:T(8,128)(2,1)S(1)} %bitcast.129, ...), kind=kOutput, calls=%fused_computation.6 | convolution fusion | flops 558366720 | bytes 27329024 | tf_op jit(solution)/shard_map/pihd,pjhd->phij/dot_general | solution.py:28
  260.6 2.6 fusion.26
  263.2 0.0 copy-start.4
  263.2 1.5 fusion.28
  264.7 0.0 copy-done.4
  264.7 1.7 pad_maximum_fusion
  266.4 0.0 copy-start.6
  266.4 0.1 copy.41
  266.5 0.0 copy-start.5
  266.5 1.3 copy-done.5
  267.8 1.5 copy-done.6
  269.3 12.4 %multiply_convert_fusion = bf16[4096,2048]{1,0:T(8,128)(2,1)} fusion(bf16[512,2048]{0,1:T(8,128)(2,1)S(1)} %bitcast.137, bf16[1,512,4096]{2,1,0:T(8,128)(2,1)S(1)} %copy-done.6), kind=kOutput, calls=%fused_computation.1 | convolution fusion | flops 8606711808 | bytes 23068672 | tf_op jit(solution)/shard_map/dot_general | solution.py:78
  281.8 0.0 reduce-scatter.2.cloned.1.call-update
  281.8 14.7 %fusion.9 = bf16[1,1,512,4096]{3,2,1,0:T(8,128)(2,1)} fusion(bf16[512,2048]{0,1:T(8,128)(2,1)} %bitcast.138, bf16[4096,2048]{1,0:T(8,128)(2,1)} %all-gather.5.cloned.1.call-done), kind=kOutput, calls=%fused_computation.14 | convolution fusion | flops 8592031744 | bytes 23068672 | tf_op jit(solution)/shard_map/dot_general | solution.py:89
  296.5 18.9 %copy.42 = bf16[1,1,512,4096]{2,1,0,3:T(2,128)(2,1)} copy(bf16[1,1,512,4096]{3,2,1,0:T(8,128)(2,1)} %fusion.9) | data formatting | bytes 8388608 | tf_op jit(solution)/shard_map/reshape | solution.py:92
  315.4 0.5 broadcast.112
  315.9 28.5 %reduce.11 = bf16[4096,512]{1,0:T(8,128)(2,1)} reduce(bf16[4096,1,1,512]{3,2,1,0:T(2,128)(2,1)} %bitcast.123, bf16[]{:T(256)} %broadcast.112), dimensions={1,2}, to_apply=%bitcast.101.reduce_sub_computation | reduce | bytes 8388610
  344.5 5.9 reshape.260
  350.4 55.6 %all_to_all.4 = bf16[2,2,524288]{2,1,0:T(2,128)(2,1)} all-to-all(bf16[2,2,524288]{2,1,0:T(2,128)(2,1)} %reshape.260), channel_id=1, replica_groups=mesh['dp'=8,'phase'=2,'mp'=2] {'mp'}, dimensions={0} | all-to-all | bytes 8388608 | tf_op jit(solution)/shard_map/all_to_all | solution.py:93
  406.0 7.1 %reshape.261 = bf16[4096,1,1,512]{3,2,1,0:T(2,128)(2,1)} reshape(bf16[2,2,524288]{2,1,0:T(2,128)(2,1)} %all_to_all.4) | data formatting | bytes 8388608
  413.2 7.7 %copy.59 = f32[1,1,512,4096]{2,3,0,1:T(8,128)} copy(bf16[1,1,512,4096]{2,1,0,3:T(2,128)(2,1)} %bitcast.125) | data formatting | bytes 12582912
  420.9 6.9 %reduce_sum.43 = f32[512,2048]{0,1:T(8,128)} reduce(f32[512,2,2048]{0,2,1:T(8,128)} %bitcast.124, f32[]{:T(128)} %constant.3.clone.1), dimensions={1}, to_apply=%region_4.5 | reduce | flops 1048576 | bytes 12582916 | tf_op jit(solution)/shard_map/reduce_sum | solution.py:94
  427.8 5.4 copy.60
  433.2 1.3 collective-permute-start.1
  434.4 127.8 %reduce-scatter.2.cloned.1.call-done = bf16[512,2048]{1,0:T(8,128)(2,1)} async-done(((bf16[4096,2048]{1,0:T(8,128)(2,1)}), bf16[512,2048]{1,0:T(8,128)(2,1)}) %reduce-scatter.2.cloned.1.call-update) | async-done | bytes 2097168 | tf_op jit(solution)/shard_map/reduce_scatter | solution.py:75
  562.2 2.9 slice.28
  565.1 1.3 collective-permute-start.2
  566.4 3.1 copy.45
  569.5 3.9 copy.46
  573.4 0.0 collective-permute-done.1
  573.4 2.8 fusion.13
  576.2 34.9 %psum.15 = f32[2048]{0:T(1024)} all-reduce(f32[2048]{0:T(1024)S(1)} %broadcast_multiply_fusion), channel_id=1, replica_groups=mesh['dp'=8,'phase'=2,'mp'=2] {'dp','phase'}, use_global_device_ids=true, to_apply=%region_7.8 | all-reduce | flops 2048 | bytes 16384 | tf_op jit(solution)/shard_map/psum | solution.py:98
  611.1 0.0 copy-start.3
  611.1 4.4 fusion.22
  615.6 0.0 copy-done.3
  615.6 0.5 convert_element_type.128
  616.1 0.0 collective-permute-done.2
  616.1 3.2 slice_select_fusion
  (4 shorter events, 0.0 us)
Async XLA Ops:
  7.2 74.9 %all-gather.3.cloned.1.call-start = ((), (), s32[]{:S(2)}) async-start(), calls=%async_computation.2 | async-start | bytes 6291456 | tf_op jit(solution)/shard_map/all_gather | solution.py:59
  10.0 14.2 %copy-start = (bf16[1,1,512,2048]{3,2,1,0:T(8,128)(2,1)S(1)}, bf16[1,1,512,2048]{3,2,1,0:T(8,128)(2,1)}, u32[]{:S(2)}) copy-start(bf16[1,1,512,2048]{3,2,1,0:T(8,128)(2,1)} %param.5) | copy-start | bytes 6291460
  18.1 5.2 collective-permute-start
  23.3 187.8 %all-gather.5.cloned.1.call-start = ((), (), s32[]{:S(2)}) async-start(), calls=%async_computation.3 | async-start | bytes 17825792 | tf_op jit(solution)/shard_map/all_gather | solution.py:61
  24.1 538.1 %reduce-scatter.2.cloned.1.call-start = ((), (), s32[]{:S(2)}) async-start(), calls=%async_computation.4 | async-start | bytes 18874368 | tf_op jit(solution)/shard_map/reduce_scatter | solution.py:75
  240.7 6.9 %copy-start.1 = (bf16[1,1,512,2048]{2,3,1,0:T(8,128)(2,1)S(1)}, bf16[1,1,512,2048]{2,3,1,0:T(8,128)(2,1)}, u32[]{:S(2)}) copy-start(bf16[1,1,512,2048]{2,3,1,0:T(8,128)(2,1)} %copy.33) | copy-start | bytes 6291460
  247.5 3.7 copy-start.2
  263.2 1.5 copy-start.4
  266.4 2.9 copy-start.6
  266.5 1.3 copy-start.5
  433.2 140.2 %collective-permute-start.1 = (f32[1,512,2048]{2,1,0:T(8,128)}, f32[1,512,2048]{2,1,0:T(8,128)}, u32[]{:S(2)}, u32[]{:S(2)}) collective-permute-start(f32[1,512,2048]{2,1,0:T(8,128)} %bitcast.136), channel_id=1, source_target_pairs={{2,0},{3,1},{6,4},{7,5},{10,8},{11,9},{14,12},{15,13},{18,16},{19,... | collective-permute-start | bytes 12582920 | tf_op jit(solution)/shard_map/ppermute | solution.py:14
  565.1 51.0 %collective-permute-start.2 = (f32[256,2048]{1,0:T(8,128)}, f32[256,2048]{1,0:T(8,128)}, u32[]{:S(2)}, u32[]{:S(2)}) collective-permute-start(f32[256,2048]{1,0:T(8,128)} %slice.28), channel_id=1, source_target_pairs={{2,0},{3,1},{6,4},{7,5},{10,8},{11,9},{14,12},{15,13},{18,16},{19,... | collective-permute-start | bytes 6291464 | tf_op jit(solution)/shard_map/ppermute | solution.py:14
  611.1 4.4 copy-start.3
Sparse Core Ops, SparseCore 0:
  23.5 58.5 all-gather.2
  84.2 126.8 all-gather.4
  281.9 280.2 reduce-scatter.1
where the time goes:
time: 636 us; the launch traced here: 626 us
  waiting for transfers between devices  314 us (49%)
  blocking collectives  96.5 us (15%)
  matrix products  69.8 us (11%)
  local copies, waits for them, and re-layouts  64.9 us (10%)
  other arithmetic  59.8 us (9%)
  between operations  15.5 us (2%)
    all_gather x1, waiting for transfers between devices, on_device(): whole_weight = lax.all_gather(w_kv, ('dp', 'phase'), axis=0, tiled=True)  129 us
    reduce_scatter x1, waiting for transfers between devices, on_device(): lax.psum_scatter((pair_scale * lax.dot_general(enc_rows, grad_kv, (((0,),...  128 us
    all_to_all x1, blocking collectives, on_device(): lax.all_to_all(partial_enc, 'mp', split_axis=3, concat_axis=0, tiled=True)  55.6 us
    all_gather x1, waiting for transfers between devices, on_device(): enc_full = lax.all_gather(enc_moved, 'mp', axis=2, tiled=True)  54.1 us
    psum x1, blocking collectives, on_device(): d_gain = lax.psum(gain_term, ('dp', 'phase'))  34.9 us
    unnamed x20, local copies, waits for them, and re-layouts  32 us
    unnamed x1, other arithmetic  28.5 us
    reshape x1, local copies, waits for them, and re-layouts, on_device(): partial_enc = partial_enc.reshape(1, pair_dev, length, D)  18.9 us
  transfers between devices with their start and end apart: 6, of which 4 were waited for; matrix products, arithmetic and copies ran while one was open for 19% of the time, Pallas kernels for 0%

commit v1 on v0

--- a/solution.py
+++ b/solution.py
@@ -95,7 +95,9 @@
     grad_enc = shifted(summed, "phase", -1)
     grad_normed = grad_enc * gain_wide
     gain_term = pair_scale * jnp.sum(grad_enc * normed, axis=(0, 1))
-    d_gain = lax.psum(gain_term, ("dp", "phase"))
+    d_gain = gain_term
+    for src_i in ("phase", "dp"):
+        d_gain = lax.psum(d_gain, src_i)
     sec_grads = jnp.where(section == 0, grad_normed.astype(bf16), dec_grads)[None]
     return (sec_grads, d_wkv, d_gain)
 

time: 636 us -> 626 us (0.984)
  blocking collectives: 96.5 us -> 86.5 us
    psum x1 -> x2, blocking collectives: 34.9 us -> 24.9 us  [on_device(): d_gain = lax.psum(d_gain, src_i)]
where the time goes in v1:
time: 626 us; the launch traced here: 616 us
  waiting for transfers between devices  314 us (50%)
  blocking collectives  86.5 us (14%)
  matrix products  69.8 us (11%)
  local copies, waits for them, and re-layouts  64.9 us (10%)
  other arithmetic  59.8 us (10%)
  between operations  15.5 us (2%)
    all_gather x1, waiting for transfers between devices, on_device(): whole_weight = lax.all_gather(w_kv, ('dp', 'phase'), axis=0, tiled=True)  129 us
    reduce_scatter x1, waiting for transfers between devices, on_device(): lax.psum_scatter((pair_scale * lax.dot_general(enc_rows, grad_kv, (((0,),...  128 us
    all_to_all x1, blocking collectives, on_device(): lax.all_to_all(partial_enc, 'mp', split_axis=3, concat_axis=0, tiled=True)  55.6 us
    all_gather x1, waiting for transfers between devices, on_device(): enc_full = lax.all_gather(enc_moved, 'mp', axis=2, tiled=True)  54.1 us
    unnamed x20, local copies, waits for them, and re-layouts  32 us
    unnamed x1, other arithmetic  28.5 us
    psum x2, blocking collectives, on_device(): d_gain = lax.psum(d_gain, src_i)  24.9 us
    reshape x1, local copies, waits for them, and re-layouts, on_device(): partial_enc = partial_enc.reshape(1, pair_dev, length, D)  18.9 us
  transfers between devices with their start and end apart: 6, of which 4 were waited for; matrix products, arithmetic and copies ran while one was open for 19% of the time, Pallas kernels for 0%

profile of v1, /device:TPU:0, one launch (start us, length us, event | category | flops | bytes accessed | tf_op | source)
XLA Modules:
  0.0 616.0 jit_solution(10454734353962807017)
XLA Ops:
  7.2 0.0 all-gather.3.cloned.1.call-start
  7.2 0.7 convert_element_type.108
  7.9 2.1 fusion.14
  10.0 6.0 psum.21
  16.0 2.1 fusion.12
  18.1 2.7 collective-permute-start
  20.8 2.5 collective-permute-done
  23.3 0.0 all-gather.3.cloned.1.call-update
  23.3 0.0 all-gather.5.cloned.1.call-start
  23.4 0.7 all-gather.5.cloned.1.call-update
  24.1 0.0 reduce-scatter.2.cloned.1.call-start
  24.1 0.0 copy-done
  24.1 2.5 copy.33
  28.0 54.1 %all-gather.3.cloned.1.call-done = bf16[1,512,4096]{2,1,0:T(8,128)(2,1)} async-done(((bf16[1,512,2048]{2,1,0:T(8,128)(2,1)}), bf16[1,512,4096]{2,1,0:T(8,128)(2,1)}) %all-gather.3.cloned.1.call-update) | async-done | bytes 4194320 | tf_op jit(solution)/shard_map/all_gather | solution.py:59
  82.1 129.1 %all-gather.5.cloned.1.call-done = bf16[4096,2048]{1,0:T(8,128)(2,1)} async-done(((bf16[256,2048]{1,0:T(8,128)(2,1)}), bf16[4096,2048]{1,0:T(8,128)(2,1)}) %all-gather.5.cloned.1.call-update) | async-done | bytes 16777232 | tf_op jit(solution)/shard_map/all_gather | solution.py:61
  211.2 14.5 %fusion.18 = bf16[512,2048]{1,0:T(8,128)(2,1)} fusion(bf16[4096,2048]{1,0:T(8,128)(2,1)} %all-gather.5.cloned.1.call-done, bf16[1,512,4096]{2,1,0:T(8,128)(2,1)} %all-gather.3.cloned.1.call-done), kind=kOutput, calls=%fused_computation.26 | convolution fusion | flops 8590983168 | bytes 23068672 | tf_op jit(solution)/shard_map/dot_general | solution.py:62
  225.7 3.9 copy.31
  229.6 11.0 %fusion.39 = (f32[16,512]{1,0:T(8,128)S(1)}, f32[16,512,512]{1,2,0:T(8,128)}) fusion(pred[512]{0:T(512)(128)(4,1)S(1)} %iota_compare_fusion.1, bf16[1,512,16,2,64]{1,4,3,2,0:T(8,128)(2,1)} %bitcast.131, bf16[1,512,16,2,64]{1,4,3,2,0:T(8,128)(2,1)} %bitcast.126), kind=kOutput, calls=%fused_computation.57 | convolution fusion | flops 553648640 | bytes 18907648 | tf_op jit(solution)/shard_map/sub | solution.py:24
  240.7 0.0 copy-start.1
  240.7 6.8 %fusion.8 = bf16[16,512,512]{1,2,0:T(8,128)(2,1)S(1)} fusion(f32[16,512,512]{1,2,0:T(8,128)} %get-tuple-element.9, f32[16,512]{1,0:T(8,128)S(1)} %get-tuple-element.8), kind=kLoop, calls=%fused_computation.12 | loop fusion | flops 8388608 | bytes 25198592 | tf_op jit(solution)/shard_map/convert_element_type | solution.py:26
  247.5 0.0 copy-done.1
  247.5 0.0 copy-start.2
  247.5 3.6 fusion.27
  251.2 0.0 copy-done.2
  251.2 1.5 fusion.23
  252.7 7.8 %multiply_convert_fusion.1 = bf16[16,512,512]{1,2,0:T(8,128)(2,1)S(1)} fusion(f32[16,512]{1,0:T(8,128)S(1)} %fusion.23, f32[16,512,512]{1,2,0:T(8,128)} %get-tuple-element.9, f32[16,512]{1,0:T(8,128)S(1)} %get-tuple-element.8, bf16[1,512,16,2,64]{1,4,3,2,0:T(8,128)(2,1)S(1)} %bitcast.133, bf16[1,512,16,2,64]{1,4,3,2,0:T(8,128)(2,1)S(1)} %bitcast.129, ...), kind=kOutput, calls=%fused_computation.6 | convolution fusion | flops 558366720 | bytes 27329024 | tf_op jit(solution)/shard_map/pihd,pjhd->phij/dot_general | solution.py:28
  260.6 2.6 fusion.26
  263.2 0.0 copy-start.4
  263.2 1.5 fusion.28
  264.7 0.0 copy-done.4
  264.7 1.7 pad_maximum_fusion
  266.4 0.0 copy-start.6
  266.4 0.1 copy.41
  266.5 0.0 copy-start.5
  266.5 1.3 copy-done.5
  267.8 1.5 copy-done.6
  269.3 12.4 %multiply_convert_fusion = bf16[4096,2048]{1,0:T(8,128)(2,1)} fusion(bf16[512,2048]{0,1:T(8,128)(2,1)S(1)} %bitcast.137, bf16[1,512,4096]{2,1,0:T(8,128)(2,1)S(1)} %copy-done.6), kind=kOutput, calls=%fused_computation.1 | convolution fusion | flops 8606711808 | bytes 23068672 | tf_op jit(solution)/shard_map/dot_general | solution.py:78
  281.8 0.0 reduce-scatter.2.cloned.1.call-update
  281.8 14.7 %fusion.9 = bf16[1,1,512,4096]{3,2,1,0:T(8,128)(2,1)} fusion(bf16[512,2048]{0,1:T(8,128)(2,1)} %bitcast.138, bf16[4096,2048]{1,0:T(8,128)(2,1)} %all-gather.5.cloned.1.call-done), kind=kOutput, calls=%fused_computation.14 | convolution fusion | flops 8592031744 | bytes 23068672 | tf_op jit(solution)/shard_map/dot_general | solution.py:89
  296.5 18.9 %copy.42 = bf16[1,1,512,4096]{2,1,0,3:T(2,128)(2,1)} copy(bf16[1,1,512,4096]{3,2,1,0:T(8,128)(2,1)} %fusion.9) | data formatting | bytes 8388608 | tf_op jit(solution)/shard_map/reshape | solution.py:92
  315.4 0.5 broadcast.112
  315.9 28.5 %reduce.11 = bf16[4096,512]{1,0:T(8,128)(2,1)} reduce(bf16[4096,1,1,512]{3,2,1,0:T(2,128)(2,1)} %bitcast.123, bf16[]{:T(256)} %broadcast.112), dimensions={1,2}, to_apply=%bitcast.101.reduce_sub_computation | reduce | bytes 8388610
  344.5 5.9 reshape.260
  350.4 55.6 %all_to_all.4 = bf16[2,2,524288]{2,1,0:T(2,128)(2,1)} all-to-all(bf16[2,2,524288]{2,1,0:T(2,128)(2,1)} %reshape.260), channel_id=1, replica_groups=mesh['dp'=8,'phase'=2,'mp'=2] {'mp'}, dimensions={0} | all-to-all | bytes 8388608 | tf_op jit(solution)/shard_map/all_to_all | solution.py:93
  406.0 7.1 %reshape.261 = bf16[4096,1,1,512]{3,2,1,0:T(2,128)(2,1)} reshape(bf16[2,2,524288]{2,1,0:T(2,128)(2,1)} %all_to_all.4) | data formatting | bytes 8388608
  413.2 7.7 %copy.59 = f32[1,1,512,4096]{2,3,0,1:T(8,128)} copy(bf16[1,1,512,4096]{2,1,0,3:T(2,128)(2,1)} %bitcast.125) | data formatting | bytes 12582912
  420.9 6.9 %reduce_sum.43 = f32[512,2048]{0,1:T(8,128)} reduce(f32[512,2,2048]{0,2,1:T(8,128)} %bitcast.124, f32[]{:T(128)} %constant.3.clone.1), dimensions={1}, to_apply=%region_4.5 | reduce | flops 1048576 | bytes 12582916 | tf_op jit(solution)/shard_map/reduce_sum | solution.py:94
  427.8 5.4 copy.60
  433.2 1.3 collective-permute-start.1
  434.4 127.8 %reduce-scatter.2.cloned.1.call-done = bf16[512,2048]{1,0:T(8,128)(2,1)} async-done(((bf16[4096,2048]{1,0:T(8,128)(2,1)}), bf16[512,2048]{1,0:T(8,128)(2,1)}) %reduce-scatter.2.cloned.1.call-update) | async-done | bytes 2097168 | tf_op jit(solution)/shard_map/reduce_scatter | solution.py:75
  562.2 2.9 slice.28
  565.1 1.3 collective-permute-start.2
  566.4 3.1 copy.45
  569.5 3.9 copy.46
  573.4 0.0 collective-permute-done.1
  573.4 2.8 fusion.13
  576.2 4.6 psum.22
  580.8 20.3 %psum.23 = f32[2048]{0:T(1024)} all-reduce(f32[2048]{0:T(1024)S(1)} %psum.22), channel_id=1, replica_groups=mesh['dp'=8,'phase'=2,'mp'=2] {'dp'}, use_global_device_ids=true, to_apply=%region_8.9 | all-reduce | flops 2048 | bytes 16384 | tf_op jit(solution)/shard_map/psum | solution.py:100
  601.1 0.0 copy-start.3
  601.1 4.4 fusion.22
  605.5 0.0 copy-done.3
  605.5 0.5 convert_element_type.128
  606.0 0.0 collective-permute-done.2
  606.0 3.2 slice_select_fusion
  (5 shorter events, 0.0 us)
Async XLA Ops:
  7.2 74.9 %all-gather.3.cloned.1.call-start = ((), (), s32[]{:S(2)}) async-start(), calls=%async_computation.2 | async-start | bytes 6291456 | tf_op jit(solution)/shard_map/all_gather | solution.py:59
  10.0 14.2 %copy-start = (bf16[1,1,512,2048]{3,2,1,0:T(8,128)(2,1)S(1)}, bf16[1,1,512,2048]{3,2,1,0:T(8,128)(2,1)}, u32[]{:S(2)}) copy-start(bf16[1,1,512,2048]{3,2,1,0:T(8,128)(2,1)} %param.5) | copy-start | bytes 6291460
  18.1 5.2 collective-permute-start
  23.3 187.8 %all-gather.5.cloned.1.call-start = ((), (), s32[]{:S(2)}) async-start(), calls=%async_computation.3 | async-start | bytes 17825792 | tf_op jit(solution)/shard_map/all_gather | solution.py:61
  24.1 538.1 %reduce-scatter.2.cloned.1.call-start = ((), (), s32[]{:S(2)}) async-start(), calls=%async_computation.4 | async-start | bytes 18874368 | tf_op jit(solution)/shard_map/reduce_scatter | solution.py:75
  240.7 6.9 %copy-start.1 = (bf16[1,1,512,2048]{2,3,1,0:T(8,128)(2,1)S(1)}, bf16[1,1,512,2048]{2,3,1,0:T(8,128)(2,1)}, u32[]{:S(2)}) copy-start(bf16[1,1,512,2048]{2,3,1,0:T(8,128)(2,1)} %copy.33) | copy-start | bytes 6291460
  247.5 3.7 copy-start.2
  263.2 1.5 copy-start.4
  266.4 2.9 copy-start.6
  266.5 1.3 copy-start.5
  433.2 140.2 %collective-permute-start.1 = (f32[1,512,2048]{2,1,0:T(8,128)}, f32[1,512,2048]{2,1,0:T(8,128)}, u32[]{:S(2)}, u32[]{:S(2)}) collective-permute-start(f32[1,512,2048]{2,1,0:T(8,128)} %bitcast.136), channel_id=1, source_target_pairs={{2,0},{3,1},{6,4},{7,5},{10,8},{11,9},{14,12},{15,13},{18,16},{19,... | collective-permute-start | bytes 12582920 | tf_op jit(solution)/shard_map/ppermute | solution.py:14
  565.1 41.0 %collective-permute-start.2 = (f32[256,2048]{1,0:T(8,128)}, f32[256,2048]{1,0:T(8,128)}, u32[]{:S(2)}, u32[]{:S(2)}) collective-permute-start(f32[256,2048]{1,0:T(8,128)} %slice.28), channel_id=1, source_target_pairs={{2,0},{3,1},{6,4},{7,5},{10,8},{11,9},{14,12},{15,13},{18,16},{19,... | collective-permute-start | bytes 6291464 | tf_op jit(solution)/shard_map/ppermute | solution.py:14
  601.1 4.4 copy-start.3
Sparse Core Ops, SparseCore 0:
  23.5 58.5 all-gather.2
  84.2 126.8 all-gather.4
  281.9 280.2 reduce-scatter.1
